TPU v7x, 512 devices: a whole 4x4x16 slice. The times are simulated.
512 devices in a mesh: bx: 16 (over x_lo, y, core), by: 32 (over z, x_hi).
Axes of the slice: x: 4 (x_hi: 2, x_lo: 2; x = x_hi * 2 + x_lo), y: 4, z: 16, core: 2. Of those that a mesh axis runs over, the one named last changes fastest.
Arguments:
- solution: float32 [4, 2048, 2048], P(None, 'by', 'bx'), may hold values from -6 to 6
- source: float32 [4, 2048, 2048], P(None, 'by', 'bx'), may hold values from -12 to 12
- class_ids: int32 [4, 2048, 2048], P(None, 'by', 'bx'), may hold values from 0 to 7
- conductivity: float32 [8], replicated, may hold values from 0.3 to 3
- spacing_x: float32 [2048], P('bx'), may hold values from 0.7 to 1.4
- spacing_y: float32 [2048], P('by'), may hold values from 0.7 to 1.4
- spacing_z: float32 [4], replicated, may hold values from 0.7 to 1.4
- forward_x: bfloat16 [2048, 2048], P('bx'), may hold values from -0.125 to 0.125
- forward_y: bfloat16 [2048, 2048], P('by'), may hold values from -0.125 to 0.125
- forward_z: bfloat16 [4, 4], replicated, may hold values from -3 to 3
- inverse_x: bfloat16 [2048, 2048], P('bx'), may hold values from -0.125 to 0.125
- inverse_y: bfloat16 [2048, 2048], P('by'), may hold values from -0.125 to 0.125
- inverse_z: bfloat16 [4, 4], replicated, may hold values from -3 to 3
- eigen_x: float32 [2048], P('bx'), may hold values from 0.05 to 4
- eigen_y: float32 [2048], P('by'), may hold values from 0.05 to 4
- eigen_z: float32 [4], replicated, may hold values from 0.05 to 4
Outputs:
- corrected: float32 [4, 2048, 2048], P(None, 'by', 'bx')
All inputs are finite; a program needn't handle non-finite values.
Results may differ from a plain program's by a relative error of at most 0.0039.
Values may be sent and summed in bfloat16 or wider, within the bound.
A program may use at most 64 MiB of HBM per device.

v0:
```python
import jax
import jax.numpy as jnp
from jax import lax
from jax.sharding import Mesh
from jax.sharding import PartitionSpec as P

CLASSES = 8
BY = ("by_0", "by_1")
shift_value = 0.1


def with_halo(value, sides, width):
    edges = {}
    for axis, dim in sides:
        size, length = (lax.axis_size(axis), value.shape[dim])
        up = [(i, (i + 1) % size) for i in range(size - 1)]
        last = lax.slice_in_dim(value, length - width, length, axis=dim)
        first = lax.slice_in_dim(value, 0, width, axis=dim)
        edges[dim] = (
            lax.ppermute(last, axis, up),
            lax.ppermute(first, axis, [(b, a) for a, b in up]),
        )
    done = []
    for _, dim in sides:
        low, high = edges[dim]
        around = [(width, width) if d in done else (0, 0) for d in range(value.ndim)]
        value = jnp.concatenate([jnp.pad(low, around), value, jnp.pad(high, around)], axis=dim)
        done.append(dim)
    return value


def whole_of(value, axes, dim):
    filled = value
    for number in range(len(axes) - 1, -1, -1):
        filled = lax.all_gather(filled, axes[number], axis=dim, tiled=True)
    return filled


def coefficients(class_ids, conductivity):
    result = jnp.zeros(class_ids.shape, jnp.float32)
    for index in range(CLASSES):
        result = result + jnp.where(class_ids == index, conductivity[index], jnp.float32(0.0))
    return result


def operate(solution, coef):
    stacked = jnp.stack([solution, coef])
    padded = with_halo(stacked, (("bx", 3), (BY, 2)), 1)
    padded = jnp.pad(padded, ((0, 0), (1, 1), (0, 0), (0, 0)))
    values = padded[0]
    padcoef = padded[1]
    slices = [
        (slice(2, None), slice(1, -1), slice(1, -1)),
        (slice(0, -2), slice(1, -1), slice(1, -1)),
        (slice(1, -1), slice(2, None), slice(1, -1)),
        (slice(1, -1), slice(0, -2), slice(1, -1)),
        (slice(1, -1), slice(1, -1), slice(2, None)),
        (slice(1, -1), slice(1, -1), slice(0, -2)),
    ]
    result = jnp.zeros(solution.shape, jnp.float32)
    for where_at in slices:
        neighbour = values[where_at]
        ncoef = padcoef[where_at]
        face = jnp.where(ncoef > 0, 2.0 * coef * ncoef / (coef + ncoef), coef)
        result = result + face * (solution - neighbour)
    return result


def x_high(values, matrix_rows):
    columns = matrix_rows.astype(jnp.float32)
    return jnp.einsum(
        "kjx,mx->kjm",
        lax.all_gather(values, "bx", axis=2, tiled=True),
        columns,
        precision=lax.Precision.HIGHEST,
    )


def y_low(values, matrix_rows):
    return jnp.einsum(
        "kjm,nj->knm", whole_of(values, BY, 1), matrix_rows, preferred_element_type=jnp.float32
    )


def on_device(
    solution,
    source,
    class_ids,
    conductivity,
    spacing_x,
    spacing_y,
    spacing_z,
    forward_x,
    forward_y,
    forward_z,
    inverse_x,
    inverse_y,
    inverse_z,
    eigen_x,
    eigen_y,
    eigen_z,
):
    highest = lax.Precision.HIGHEST
    coef = coefficients(class_ids, conductivity)
    operated = operate(solution, coef)
    weights = spacing_z[:, None, None] * spacing_y[None, :, None] * spacing_x[None, None, :]
    restricted = (weights * (source - operated)).astype(jnp.bfloat16)
    modes_xy = x_high(y_low(restricted, forward_y), forward_x)
    modes = jnp.einsum("qk,knm->qnm", forward_z.astype(jnp.float32), modes_xy, precision=highest)
    divisor = eigen_x[None, None, :] + eigen_y[None, :, None] + eigen_z[:, None, None] + shift_value
    scaled = modes / divisor
    spectral = jnp.einsum(
        "kq,qnm->knm", inverse_z.astype(jnp.float32), scaled, precision=highest
    ).astype(jnp.bfloat16)
    field = x_high(y_low(spectral, inverse_y), inverse_x)
    return solution + weights * field


def solution(mesh):
    split = Mesh(mesh.devices.reshape(mesh.shape["bx"], 16, 2), ("bx", "by_0", "by_1"))
    placed = (
        P(None, BY, "bx"),
        P(None, BY, "bx"),
        P(None, BY, "bx"),
        P(),
        P("bx"),
        P(BY),
        P(),
        P("bx", None),
        P(BY, None),
        P(),
        P("bx", None),
        P(BY, None),
        P(),
        P("bx"),
        P(BY),
        P(),
    )
    return jax.shard_map(
        on_device, mesh=split, in_specs=placed, out_specs=P(None, BY, "bx"), check_vma=False
    )
```

profile of v0, /device:TPU:1, one launch (start us, length us, event | category | flops | bytes accessed | tf_op | source)
XLA Modules:
  0.0 307.3 jit_solution(11412667438014760652)
XLA Ops:
  6.5 0.0 copy-start
  6.5 0.0 all-gather.5.cloned.1.call-start
  6.5 1.6 fusion.42
  8.2 0.0 copy-start.3
  8.2 0.0 copy-start.5
  8.2 0.0 copy-start.6
  8.2 6.0 %fusion.41 = f32[1,4,64,128]{3,2,1,0:T(8,128)S(1)} fusion(f32[]{:T(128)} %bitcast.8, s32[4,64,128]{2,1,0:T(8,128)} %param.18, f32[]{:T(128)} %bitcast.7, f32[]{:T(128)} %bitcast.6, f32[]{:T(128)} %bitcast.5, f32[]{:T(128)} %bitcast.4, f32[]{:T(128)} %bitcast.3, f32[]{:T(128)} %bitcast.2, f32[]{:T(128)} %bitcast.1), kind=kLoop, calls=%fused_computation.69 | loop fusion | flops 753664 | bytes 262176 | tf_op jit(solution)/shard_map/stack | solution.py:47
  14.2 1.1 fusion.14
  15.3 4.6 %collective-permute-start.1 = (f32[2,4,64,1]{3,2,1,0:T(8,128)S(1)}, f32[2,4,64,1]{3,2,1,0:T(8,128)S(1)}, u32[]{:S(2)}, u32[]{:S(2)}) collective-permute-start(f32[2,4,64,1]{3,2,1,0:T(8,128)S(1)} %get-tuple-element.7), channel_id=1, source_target_pairs={{0,32},{32,64},{64,96},{96,128},{128,160},{160,192},{192,224},{224... | collective-permute-start | bytes 6152 | tf_op jit(solution)/shard_map/ppermute | solution.py:20
  19.9 5.5 %collective-permute-start.2 = (f32[2,4,64,1]{3,2,1,0:T(8,128)S(1)}, f32[2,4,64,1]{3,2,1,0:T(8,128)S(1)}, u32[]{:S(2)}, u32[]{:S(2)}) collective-permute-start(f32[2,4,64,1]{3,2,1,0:T(8,128)S(1)} %get-tuple-element.8), channel_id=1, source_target_pairs={{32,0},{64,32},{96,64},{128,96},{160,128},{192,160},{224,192},{256... | collective-permute-start | bytes 6152 | tf_op jit(solution)/shard_map/ppermute | solution.py:21
  25.4 0.7 pad_maximum_fusion.1
  26.1 1.3 collective-permute-start
  27.4 1.3 collective-permute-start.3
  28.7 0.7 broadcast_multiply_fusion
  29.4 0.0 collective-permute-done.1
  29.5 0.0 collective-permute-done.2
  29.5 0.0 collective-permute-done
  29.5 3.9 %collective-permute-done.3 = f32[2,4,1,128]{3,2,1,0:T(1,128)S(1)} collective-permute-done((f32[2,4,1,128]{3,2,1,0:T(1,128)S(1)}, f32[2,4,1,128]{3,2,1,0:T(1,128)S(1)}, u32[]{:S(2)}, u32[]{:S(2)}) %collective-permute-start.3) | collective-permute-done | bytes 4128 | tf_op jit(solution)/shard_map/ppermute | solution.py:21
  33.4 1.2 select_maximum_fusion
  34.6 0.0 copy-start.4
  34.7 0.1 fusion.11
  34.8 0.0 copy-start.8
  34.8 0.0 copy-start.9
  34.8 5.5 %fusion.17 = bf16[4,64,128]{2,1,0:T(8,128)(2,1)S(1)} fusion(f32[4,64,128]{2,1,0:T(8,128)S(1)} %copy-done.5, f32[4,64,128]{2,1,0:T(8,128)S(1)} %copy-done.1, f32[6,66,130]{2,1,0:T(8,128)S(1)} %get-tuple-element.6, f32[6,66,130]{2,1,0:T(8,128)S(1)} %get-tuple-element.5, f32[128]{0:T(128)S(1)} %copy-done.6, f32[4,64]{1,0:T(4,128)S(1)} %broadcast_multiply_fusion, ...), kind=kLoop, calls=%fused_computation.30 | loop fusion | flops 2457600 | bytes 2033184 | tf_op jit(solution)/shard_map/convert_element_type | solution.py:107
  40.3 5.4 %all_gather.18 = bf16[4,128,128]{2,1,0:T(8,128)(2,1)} all-gather(bf16[4,64,128]{2,1,0:T(8,128)(2,1)S(1)} %fusion.17), channel_id=1, replica_groups=mesh['bx'=16,'by_0'=16,'by_1'=2] {'by_1'}, dimensions={1}, use_global_device_ids=true | all-gather | bytes 196608 | tf_op jit(solution)/shard_map/all_gather | solution.py:35
  45.7 0.0 all-gather.5.cloned.1.call-update
  45.7 0.0 copy-start.11
  45.7 0.0 copy-start.12
  45.7 0.0 all-gather.7.cloned.1.call-start
  45.8 70.4 %all-gather.5.cloned.1.call-done = bf16[4,2048,128]{2,1,0:T(8,128)(2,1)} async-done(((bf16[4,128,128]{2,1,0:T(8,128)(2,1)}), bf16[4,2048,128]{2,1,0:T(8,128)(2,1)}) %all-gather.5.cloned.1.call-update) | async-done | bytes 2097168 | tf_op jit(solution)/shard_map/all_gather | solution.py:35
  116.2 2.7 convolution_bitcast_fusion
  118.9 0.0 all-gather.7.cloned.1.call-update
  118.9 0.0 all-gather.9.cloned.1.call-start
  119.0 0.1 broadcast_add_fusion
  119.1 50.9 %all-gather.7.cloned.1.call-done = f32[4,64,2048]{2,1,0:T(8,128)} async-done(((f32[4,64,128]{2,1,0:T(8,128)}), f32[4,64,2048]{2,1,0:T(8,128)}) %all-gather.7.cloned.1.call-update) | async-done | bytes 2097168 | tf_op jit(solution)/shard_map/all_gather | solution.py:73
  170.0 2.7 fusion.9
  172.7 0.0 copy-start.2
  172.7 0.3 fusion.6
  173.1 0.2 fusion.7
  173.3 5.4 %all_gather.21 = bf16[4,128,128]{2,0,1:T(4,128)(2,1)} all-gather(bf16[4,64,128]{2,0,1:T(4,128)(2,1)S(1)} %fusion.7), channel_id=1, replica_groups=mesh['bx'=16,'by_0'=16,'by_1'=2] {'by_1'}, dimensions={1}, use_global_device_ids=true | all-gather | bytes 196608 | tf_op jit(solution)/shard_map/all_gather | solution.py:35
  178.7 0.0 all-gather.9.cloned.1.call-update
  178.7 0.0 all-gather.11.cloned.1.call-start
  178.8 64.6 %all-gather.9.cloned.1.call-done = bf16[4,2048,128]{2,0,1:T(4,128)(2,1)} async-done(((bf16[4,128,128]{2,0,1:T(4,128)(2,1)}), bf16[4,2048,128]{2,0,1:T(4,128)(2,1)}) %all-gather.9.cloned.1.call-update) | async-done | bytes 2097168 | tf_op jit(solution)/shard_map/all_gather | solution.py:35
  243.4 2.7 fusion.2
  246.1 0.0 all-gather.11.cloned.1.call-update
  246.1 51.2 %all-gather.11.cloned.1.call-done = f32[4,64,2048]{2,1,0:T(8,128)} async-done(((f32[4,64,128]{2,1,0:T(8,128)}), f32[4,64,2048]{2,1,0:T(8,128)}) %all-gather.11.cloned.1.call-update) | async-done | bytes 2097168 | tf_op jit(solution)/shard_map/all_gather | solution.py:73
  297.4 0.0 copy-done.2
  297.4 3.3 %fusion.5 = f32[4,64,128]{2,1,0:T(8,128)} fusion(f32[4,64,128]{2,1,0:T(8,128)S(1)} %copy-done.1, f32[4,64,2048]{2,1,0:T(8,128)} %all-gather.11.cloned.1.call-done, bf16[128,2048]{1,0:T(8,128)(2,1)S(1)} %copy-done.2, f32[128]{0:T(128)S(1)} %copy-done.6, f32[4,64]{1,0:T(4,128)S(1)} %broadcast_multiply_fusion), kind=kOutput, calls=%fused_computation.5 | convolution fusion | flops 805404672 | bytes 2885120 | tf_op jit(solution)/shard_map/kjx,mx->kjm/dot_general | solution.py:71
  (15 shorter events, 0.0 us)
Async XLA Ops:
  6.5 163.5 %copy-start = (bf16[128,2048]{1,0:T(8,128)(2,1)S(1)}, bf16[128,2048]{1,0:T(8,128)(2,1)}, u32[]{:S(2)}) copy-start(bf16[128,2048]{1,0:T(8,128)(2,1)} %param.23) | copy-start | bytes 1572868
  6.5 109.7 %all-gather.5.cloned.1.call-start = ((), (), s32[]{:S(2)}) async-start(), calls=%async_computation | async-start | bytes 2228224 | tf_op jit(solution)/shard_map/all_gather | solution.py:35
  8.2 26.6 %copy-start.1 = (f32[4,64,128]{2,1,0:T(8,128)S(1)}, f32[4,64,128]{2,1,0:T(8,128)}, u32[]{:S(2)}) copy-start(f32[4,64,128]{2,1,0:T(8,128)} %param.16) | copy-start | bytes 393220
  8.2 26.6 %copy-start.3 = (s32[4,64,128]{2,1,0:T(8,128)S(1)}, s32[4,64,128]{2,1,0:T(8,128)}, u32[]{:S(2)}) copy-start(s32[4,64,128]{2,1,0:T(8,128)} %param.18) | copy-start | bytes 393220
  8.2 26.6 %copy-start.5 = (f32[4,64,128]{2,1,0:T(8,128)S(1)}, f32[4,64,128]{2,1,0:T(8,128)}, u32[]{:S(2)}) copy-start(f32[4,64,128]{2,1,0:T(8,128)} %param.17) | copy-start | bytes 393220
  8.2 26.6 %copy-start.6 = (f32[128]{0:T(128)S(1)}, f32[128]{0:T(128)}, u32[]{:S(2)}) copy-start(f32[128]{0:T(128)} %param.20) | copy-start | bytes 1540
  15.3 14.2 %collective-permute-start.1 = (f32[2,4,64,1]{3,2,1,0:T(8,128)S(1)}, f32[2,4,64,1]{3,2,1,0:T(8,128)S(1)}, u32[]{:S(2)}, u32[]{:S(2)}) collective-permute-start(f32[2,4,64,1]{3,2,1,0:T(8,128)S(1)} %get-tuple-element.7), channel_id=1, source_target_pairs={{0,32},{32,64},{64,96},{96,128},{128,160},{160,192},{192,224},{224... | collective-permute-start | bytes 6152 | tf_op jit(solution)/shard_map/ppermute | solution.py:20
  19.9 9.6 %collective-permute-start.2 = (f32[2,4,64,1]{3,2,1,0:T(8,128)S(1)}, f32[2,4,64,1]{3,2,1,0:T(8,128)S(1)}, u32[]{:S(2)}, u32[]{:S(2)}) collective-permute-start(f32[2,4,64,1]{3,2,1,0:T(8,128)S(1)} %get-tuple-element.8), channel_id=1, source_target_pairs={{32,0},{64,32},{96,64},{128,96},{160,128},{192,160},{224,192},{256... | collective-permute-start | bytes 6152 | tf_op jit(solution)/shard_map/ppermute | solution.py:21
  26.1 3.3 %collective-permute-start = (f32[2,4,1,128]{3,2,1,0:T(1,128)S(1)}, f32[2,4,1,128]{3,2,1,0:T(1,128)S(1)}, u32[]{:S(2)}, u32[]{:S(2)}) collective-permute-start(f32[2,4,1,128]{3,2,1,0:T(1,128)S(1)} %get-tuple-element.9), channel_id=1, source_target_pairs={{0,1},{1,2},{2,3},{3,4},{4,5},{5,6},{6,7},{7,8},{8,9},{9,10},{10,1... | collective-permute-start | bytes 12296 | tf_op jit(solution)/shard_map/ppermute | solution.py:20
  27.4 6.0 %collective-permute-start.3 = (f32[2,4,1,128]{3,2,1,0:T(1,128)S(1)}, f32[2,4,1,128]{3,2,1,0:T(1,128)S(1)}, u32[]{:S(2)}, u32[]{:S(2)}) collective-permute-start(f32[2,4,1,128]{3,2,1,0:T(1,128)S(1)} %get-tuple-element.10), channel_id=1, source_target_pairs={{1,0},{2,1},{3,2},{4,3},{5,4},{6,5},{7,6},{8,7},{9,8},{10,9},{11,1... | collective-permute-start | bytes 12296 | tf_op jit(solution)/shard_map/ppermute | solution.py:21
  34.6 81.6 %copy-start.4 = (bf16[64,2048]{1,0:T(8,128)(2,1)S(1)}, bf16[64,2048]{1,0:T(8,128)(2,1)}, u32[]{:S(2)}) copy-start(bf16[64,2048]{1,0:T(8,128)(2,1)} %param.24) | copy-start | bytes 786436
  34.8 84.2 %copy-start.8 = (f32[64]{0:T(128)S(1)}, f32[64]{0:T(128)}, u32[]{:S(2)}) copy-start(f32[64]{0:T(128)} %param.30) | copy-start | bytes 772
  34.8 84.2 %copy-start.9 = (f32[128]{0:T(128)S(1)}, f32[128]{0:T(128)}, u32[]{:S(2)}) copy-start(f32[128]{0:T(128)} %param.29) | copy-start | bytes 1540
  45.7 127.0 %copy-start.11 = (bf16[4,4]{1,0:T(4,128)(2,1)S(1)}, bf16[4,4]{1,0:T(4,128)(2,1)}, u32[]{:S(2)}) copy-start(bf16[4,4]{1,0:T(4,128)(2,1)} %param.25) | copy-start | bytes 100
  45.7 127.0 %copy-start.12 = (f32[4]{0:T(128)S(1)}, f32[4]{0:T(128)}, u32[]{:S(2)}) copy-start(f32[4]{0:T(128)} %param.31) | copy-start | bytes 52
  45.7 124.3 %all-gather.7.cloned.1.call-start = ((), (), s32[]{:S(2)}) async-start(), calls=%async_computation.1 | async-start | bytes 2228224 | tf_op jit(solution)/shard_map/all_gather | solution.py:73
  118.9 54.1 %copy-start.7 = (bf16[4,4]{1,0:T(4,128)(2,1)S(1)}, bf16[4,4]{1,0:T(4,128)(2,1)}, u32[]{:S(2)}) copy-start(bf16[4,4]{1,0:T(4,128)(2,1)} %param.28) | copy-start | bytes 100
  118.9 124.4 %all-gather.9.cloned.1.call-start = ((), (), s32[]{:S(2)}) async-start(), calls=%async_computation.2 | async-start | bytes 2228224 | tf_op jit(solution)/shard_map/all_gather | solution.py:35
  119.1 124.3 %copy-start.10 = (bf16[64,2048]{1,0:T(8,128)(2,1)S(1)}, bf16[64,2048]{1,0:T(8,128)(2,1)}, u32[]{:S(2)}) copy-start(bf16[64,2048]{1,0:T(8,128)(2,1)} %param.27) | copy-start | bytes 786436
  172.7 124.7 %copy-start.2 = (bf16[128,2048]{1,0:T(8,128)(2,1)S(1)}, bf16[128,2048]{1,0:T(8,128)(2,1)}, u32[]{:S(2)}) copy-start(bf16[128,2048]{1,0:T(8,128)(2,1)} %param.26) | copy-start | bytes 1572868
  178.7 118.7 %all-gather.11.cloned.1.call-start = ((), (), s32[]{:S(2)}) async-start(), calls=%async_computation.3 | async-start | bytes 2228224 | tf_op jit(solution)/shard_map/all_gather | solution.py:73
Sparse Core Ops, SparseCore 0:
  45.8 70.3 all-gather.4
  119.1 50.8 all-gather.6
  178.8 64.4 all-gather.8
  246.3 51.0 all-gather.10
where the time goes:
time: 308 us; the launch traced here: 307 us
  waiting for transfers between devices  241 us (78%)
  other arithmetic  15.4 us (5%)
  between operations  13.4 us (4%)
  starting transfers between devices  12.8 us (4%)
  matrix products  12 us (4%)
  blocking collectives  10.8 us (4%)
    all_gather x2, waiting for transfers between devices, whole_of(): filled = lax.all_gather(filled, axes[number], axis=dim, tiled=True)  135 us
    all_gather x2, waiting for transfers between devices, x_high(): lax.all_gather(values, 'bx', axis=2, tiled=True)  102 us
    all_gather x2, blocking collectives, whole_of(): filled = lax.all_gather(filled, axes[number], axis=dim, tiled=True)  10.8 us
    another operation x2, other arithmetic, operate(): stacked = jnp.stack([solution, coef])  7.09 us
    ppermute x2, starting transfers between devices, with_halo(): lax.ppermute(first, axis, [(b, a) for a, b in up])  6.76 us
  transfers between devices with their start and end apart: 8, of which 5 were waited for; matrix products, arithmetic and copies ran while one was open for 1% of the time, Pallas kernels for 0%

commit v1 on v0

--- a/solution.py
+++ b/solution.py
@@ -70,7 +70,9 @@
     columns = matrix_rows.astype(jnp.float32)
     return jnp.einsum(
         "kjx,mx->kjm",
-        lax.all_gather(values, "bx", axis=2, tiled=True),
+        jnp.concatenate(
+            lax.all_to_all(jnp.stack([values] * lax.axis_size("bx")), "bx", 0, 0), axis=2
+        ),
         columns,
         precision=lax.Precision.HIGHEST,
     )

time: 308 us -> 285 us (0.925)
  waiting for transfers between devices: 241 us -> 164 us
  blocking collectives: 10.8 us -> 52.3 us
  starting transfers between devices: 12.8 us -> 27.7 us
  matrix products: 12 us -> 7.57 us
    all_gather x2 -> x0, waiting for transfers between devices: 102 us -> none  [x_high(): lax.all_gather(values, 'bx', axis=2, tiled=True)]
    all_to_all x0 -> x1, blocking collectives: none -> 41.5 us  [x_high(): lax.all_to_all(jnp.stack([values] * lax.axis_size('bx')), 'bx', 0, 0)]
    all_to_all x0 -> x1, waiting for transfers between devices: none -> 27.4 us  [x_high(): lax.all_to_all(jnp.stack([values] * lax.axis_size('bx')), 'bx', 0, 0)]
    all_to_all x0 -> x1, starting transfers between devices: none -> 15.1 us  [x_high(): lax.all_to_all(jnp.stack([values] * lax.axis_size('bx')), 'bx', 0, 0)]
    dot_general x2, matrix products: 6 us -> 2.85 us  [x_high(): jnp.einsum('kjx,mx->kjm', jnp.concatenate(lax.all_to_all(jnp.stack([value...]
  transfers between devices with their start and end apart: 8 -> 7, of which waited for: 5 -> 4; matrix products, arithmetic and copies ran while one was open for 1% -> 1% of each run, Pallas kernels for 0% -> 0%
where the time goes in v1:
time: 285 us
  waiting for transfers between devices  164 us (58%)
  blocking collectives  52.3 us (18%)
  starting transfers between devices  27.7 us (10%)
  other arithmetic  15.6 us (5%)
  between operations  13.6 us (5%)
  matrix products  7.57 us (3%)
  local copies, waits for them, and re-layouts  3.6 us (1%)
    all_gather x2, waiting for transfers between devices, whole_of(): filled = lax.all_gather(filled, axes[number], axis=dim, tiled=True)  133 us
    all_to_all x1, blocking collectives, x_high(): lax.all_to_all(jnp.stack([values] * lax.axis_size('bx')), 'bx', 0, 0)  41.5 us
    all_to_all x1, waiting for transfers between devices, x_high(): lax.all_to_all(jnp.stack([values] * lax.axis_size('bx')), 'bx', 0, 0)  27.4 us
    all_to_all x1, starting transfers between devices, x_high(): lax.all_to_all(jnp.stack([values] * lax.axis_size('bx')), 'bx', 0, 0)  15.1 us
    all_gather x2, blocking collectives, whole_of(): filled = lax.all_gather(filled, axes[number], axis=dim, tiled=True)  10.8 us
    another operation x2, other arithmetic, operate(): stacked = jnp.stack([solution, coef])  7.24 us
    ppermute x2, starting transfers between devices, with_halo(): lax.ppermute(first, axis, [(b, a) for a, b in up])  6.76 us
    ppermute x2, starting transfers between devices, with_halo(): lax.ppermute(last, axis, up)  5.86 us
  transfers between devices with their start and end apart: 7, of which 4 were waited for; matrix products, arithmetic and copies ran while one was open for 1% of the time, Pallas kernels for 0%

profile of v1, /device:TPU:1, one launch (start us, length us, event | category | flops | bytes accessed | tf_op | source)
XLA Modules:
  0.0 284.6 jit_solution(11281936773659554815)
XLA Ops:
  6.5 0.0 copy-start
  6.5 0.0 all-gather.3.cloned.1.call-start
  6.5 1.6 fusion.52
  8.2 0.0 copy-start.3
  8.2 0.0 copy-start.5
  8.2 0.0 copy-start.6
  8.2 6.1 %fusion.51 = f32[1,4,64,128]{3,2,1,0:T(8,128)S(1)} fusion(f32[]{:T(128)} %bitcast.8, s32[4,64,128]{2,1,0:T(8,128)} %param.18, f32[]{:T(128)} %bitcast.7, f32[]{:T(128)} %bitcast.6, f32[]{:T(128)} %bitcast.5, f32[]{:T(128)} %bitcast.4, f32[]{:T(128)} %bitcast.3, f32[]{:T(128)} %bitcast.2, f32[]{:T(128)} %bitcast.1), kind=kLoop, calls=%fused_computation.74 | loop fusion | flops 753664 | bytes 262176 | tf_op jit(solution)/shard_map/stack | solution.py:47
  14.3 1.1 fusion.24
  15.5 4.6 %collective-permute-start.1 = (f32[2,4,64,1]{3,2,1,0:T(8,128)S(1)}, f32[2,4,64,1]{3,2,1,0:T(8,128)S(1)}, u32[]{:S(2)}, u32[]{:S(2)}) collective-permute-start(f32[2,4,64,1]{3,2,1,0:T(8,128)S(1)} %get-tuple-element.7), channel_id=1, source_target_pairs={{0,32},{32,64},{64,96},{96,128},{128,160},{160,192},{192,224},{224... | collective-permute-start | bytes 6152 | tf_op jit(solution)/shard_map/ppermute | solution.py:20
  20.1 5.5 %collective-permute-start.2 = (f32[2,4,64,1]{3,2,1,0:T(8,128)S(1)}, f32[2,4,64,1]{3,2,1,0:T(8,128)S(1)}, u32[]{:S(2)}, u32[]{:S(2)}) collective-permute-start(f32[2,4,64,1]{3,2,1,0:T(8,128)S(1)} %get-tuple-element.8), channel_id=1, source_target_pairs={{32,0},{64,32},{96,64},{128,96},{160,128},{192,160},{224,192},{256... | collective-permute-start | bytes 6152 | tf_op jit(solution)/shard_map/ppermute | solution.py:21
  25.5 0.7 pad_maximum_fusion.1
  26.3 1.3 collective-permute-start
  27.6 1.3 collective-permute-start.3
  28.9 0.7 broadcast_multiply_fusion
  29.6 0.0 collective-permute-done.1
  29.6 0.0 collective-permute-done.2
  29.6 0.0 collective-permute-done
  29.6 3.9 %collective-permute-done.3 = f32[2,4,1,128]{3,2,1,0:T(1,128)S(1)} collective-permute-done((f32[2,4,1,128]{3,2,1,0:T(1,128)S(1)}, f32[2,4,1,128]{3,2,1,0:T(1,128)S(1)}, u32[]{:S(2)}, u32[]{:S(2)}) %collective-permute-start.3) | collective-permute-done | bytes 4128 | tf_op jit(solution)/shard_map/ppermute | solution.py:21
  33.6 1.2 select_maximum_fusion
  34.8 0.0 copy-start.4
  34.8 0.1 fusion.21
  34.9 0.0 copy-done.1
  34.9 0.0 copy-done.3
  34.9 5.6 %fusion.27 = bf16[4,64,128]{2,1,0:T(8,128)(2,1)S(1)} fusion(f32[4,64,128]{2,1,0:T(8,128)S(1)} %copy-done.5, f32[4,64,128]{2,1,0:T(8,128)S(1)} %copy-done.1, f32[6,66,130]{2,1,0:T(8,128)S(1)} %get-tuple-element.6, f32[6,66,130]{2,1,0:T(8,128)S(1)} %get-tuple-element.5, f32[128]{0:T(128)S(1)} %copy-done.6, f32[4,64]{1,0:T(4,128)S(1)} %broadcast_multiply_fusion, ...), kind=kLoop, calls=%fused_computation.35 | loop fusion | flops 2457600 | bytes 2033184 | tf_op jit(solution)/shard_map/convert_element_type | solution.py:109
  40.5 5.4 %all_gather.12 = bf16[4,128,128]{2,1,0:T(8,128)(2,1)} all-gather(bf16[4,64,128]{2,1,0:T(8,128)(2,1)S(1)} %fusion.27), channel_id=1, replica_groups=mesh['bx'=16,'by_0'=16,'by_1'=2] {'by_1'}, dimensions={1}, use_global_device_ids=true | all-gather | bytes 196608 | tf_op jit(solution)/shard_map/all_gather | solution.py:35
  45.9 0.0 all-gather.3.cloned.1.call-update
  45.9 70.5 %all-gather.3.cloned.1.call-done = bf16[4,2048,128]{2,1,0:T(8,128)(2,1)} async-done(((bf16[4,128,128]{2,1,0:T(8,128)(2,1)}), bf16[4,2048,128]{2,1,0:T(8,128)(2,1)}) %all-gather.3.cloned.1.call-update) | async-done | bytes 2097168 | tf_op jit(solution)/shard_map/all_gather | solution.py:35
  116.5 0.0 copy-done.4
  116.5 2.1 convolution_bitcast_fusion
  118.5 1.6 stack.13
  120.1 15.1 %all-to-all-start = ((f32[16,4,64,128]{3,2,1,0:T(8,128)}), f32[16,4,64,128]{3,2,1,0:T(8,128)S(1)}, u32[]{:S(2)}, u32[]{:S(2)}) async-start(f32[16,4,64,128]{3,2,1,0:T(8,128)} %stack.13), calls=%async_computation | async-start | bytes 4194304 | tf_op jit(solution)/shard_map/all_to_all | solution.py:74
  135.2 0.0 copy-start.12
  135.2 0.0 copy-start.7
  135.2 0.0 all-gather.5.cloned.1.call-start
  135.3 0.1 broadcast_add_fusion
  135.4 27.4 %all-to-all-done = f32[16,4,64,128]{3,2,1,0:T(8,128)S(1)} async-done(((f32[16,4,64,128]{3,2,1,0:T(8,128)}), f32[16,4,64,128]{3,2,1,0:T(8,128)S(1)}, u32[]{:S(2)}, u32[]{:S(2)}) %all-to-all-start) | async-done | bytes 2097184 | tf_op jit(solution)/shard_map/all_to_all | solution.py:74
  162.8 1.1 fusion.3
  163.9 0.3 fusion.17
  164.3 0.2 fusion.18
  164.5 5.4 %all_gather.14 = bf16[4,128,128]{2,0,1:T(4,128)(2,1)} all-gather(bf16[4,64,128]{2,0,1:T(4,128)(2,1)S(1)} %fusion.18), channel_id=1, replica_groups=mesh['bx'=16,'by_0'=16,'by_1'=2] {'by_1'}, dimensions={1}, use_global_device_ids=true | all-gather | bytes 196608 | tf_op jit(solution)/shard_map/all_gather | solution.py:35
  169.9 0.0 all-gather.5.cloned.1.call-update
  169.9 62.2 %all-gather.5.cloned.1.call-done = bf16[4,2048,128]{2,0,1:T(4,128)(2,1)} async-done(((bf16[4,128,128]{2,0,1:T(4,128)(2,1)}), bf16[4,2048,128]{2,0,1:T(4,128)(2,1)}) %all-gather.5.cloned.1.call-update) | async-done | bytes 2097168 | tf_op jit(solution)/shard_map/all_gather | solution.py:35
  232.2 0.0 copy-done.10
  232.2 2.1 fusion.8
  234.2 0.2 stack.14
  234.5 0.0 copy-start.2
  234.5 41.5 %all_to_all.10 = f32[16,4,64,128]{3,2,1,0:T(8,128)S(1)} all-to-all(f32[16,4,64,128]{3,2,1,0:T(8,128)S(1)} %stack.14), channel_id=1, replica_groups=mesh['bx'=16,'by_0'=16,'by_1'=2] {'bx'}, dimensions={0} | all-to-all | bytes 4194304 | tf_op jit(solution)/shard_map/all_to_all | solution.py:74
  276.0 1.8 fusion.14
  (14 shorter events, 0.0 us)
Async XLA Ops:
  6.5 156.2 %copy-start = (bf16[128,2048]{1,0:T(8,128)(2,1)S(1)}, bf16[128,2048]{1,0:T(8,128)(2,1)}, u32[]{:S(2)}) copy-start(bf16[128,2048]{1,0:T(8,128)(2,1)} %param.23) | copy-start | bytes 1572868
  6.5 109.9 %all-gather.3.cloned.1.call-start = ((), (), s32[]{:S(2)}) async-start(), calls=%async_computation.2 | async-start | bytes 2228224 | tf_op jit(solution)/shard_map/all_gather | solution.py:35
  8.2 26.7 %copy-start.1 = (f32[4,64,128]{2,1,0:T(8,128)S(1)}, f32[4,64,128]{2,1,0:T(8,128)}, u32[]{:S(2)}) copy-start(f32[4,64,128]{2,1,0:T(8,128)} %param.16) | copy-start | bytes 393220
  8.2 26.7 %copy-start.3 = (s32[4,64,128]{2,1,0:T(8,128)S(1)}, s32[4,64,128]{2,1,0:T(8,128)}, u32[]{:S(2)}) copy-start(s32[4,64,128]{2,1,0:T(8,128)} %param.18) | copy-start | bytes 393220
  8.2 26.7 %copy-start.5 = (f32[4,64,128]{2,1,0:T(8,128)S(1)}, f32[4,64,128]{2,1,0:T(8,128)}, u32[]{:S(2)}) copy-start(f32[4,64,128]{2,1,0:T(8,128)} %param.17) | copy-start | bytes 393220
  8.2 26.7 %copy-start.6 = (f32[128]{0:T(128)S(1)}, f32[128]{0:T(128)}, u32[]{:S(2)}) copy-start(f32[128]{0:T(128)} %param.20) | copy-start | bytes 1540
  15.5 14.2 %collective-permute-start.1 = (f32[2,4,64,1]{3,2,1,0:T(8,128)S(1)}, f32[2,4,64,1]{3,2,1,0:T(8,128)S(1)}, u32[]{:S(2)}, u32[]{:S(2)}) collective-permute-start(f32[2,4,64,1]{3,2,1,0:T(8,128)S(1)} %get-tuple-element.7), channel_id=1, source_target_pairs={{0,32},{32,64},{64,96},{96,128},{128,160},{160,192},{192,224},{224... | collective-permute-start | bytes 6152 | tf_op jit(solution)/shard_map/ppermute | solution.py:20
  20.1 9.6 %collective-permute-start.2 = (f32[2,4,64,1]{3,2,1,0:T(8,128)S(1)}, f32[2,4,64,1]{3,2,1,0:T(8,128)S(1)}, u32[]{:S(2)}, u32[]{:S(2)}) collective-permute-start(f32[2,4,64,1]{3,2,1,0:T(8,128)S(1)} %get-tuple-element.8), channel_id=1, source_target_pairs={{32,0},{64,32},{96,64},{128,96},{160,128},{192,160},{224,192},{256... | collective-permute-start | bytes 6152 | tf_op jit(solution)/shard_map/ppermute | solution.py:21
  26.3 3.3 %collective-permute-start = (f32[2,4,1,128]{3,2,1,0:T(1,128)S(1)}, f32[2,4,1,128]{3,2,1,0:T(1,128)S(1)}, u32[]{:S(2)}, u32[]{:S(2)}) collective-permute-start(f32[2,4,1,128]{3,2,1,0:T(1,128)S(1)} %get-tuple-element.9), channel_id=1, source_target_pairs={{0,1},{1,2},{2,3},{3,4},{4,5},{5,6},{6,7},{7,8},{8,9},{9,10},{10,1... | collective-permute-start | bytes 12296 | tf_op jit(solution)/shard_map/ppermute | solution.py:20
  27.6 6.0 %collective-permute-start.3 = (f32[2,4,1,128]{3,2,1,0:T(1,128)S(1)}, f32[2,4,1,128]{3,2,1,0:T(1,128)S(1)}, u32[]{:S(2)}, u32[]{:S(2)}) collective-permute-start(f32[2,4,1,128]{3,2,1,0:T(1,128)S(1)} %get-tuple-element.10), channel_id=1, source_target_pairs={{1,0},{2,1},{3,2},{4,3},{5,4},{6,5},{7,6},{8,7},{9,8},{10,9},{11,1... | collective-permute-start | bytes 12296 | tf_op jit(solution)/shard_map/ppermute | solution.py:21
  34.8 81.7 %copy-start.4 = (bf16[64,2048]{1,0:T(8,128)(2,1)S(1)}, bf16[64,2048]{1,0:T(8,128)(2,1)}, u32[]{:S(2)}) copy-start(bf16[64,2048]{1,0:T(8,128)(2,1)} %param.24) | copy-start | bytes 786436
  120.1 15.1 %copy-start.8 = (f32[64]{0:T(128)S(1)}, f32[64]{0:T(128)}, u32[]{:S(2)}) copy-start(f32[64]{0:T(128)} %param.30) | copy-start | bytes 772
  120.1 15.1 %copy-start.9 = (f32[128]{0:T(128)S(1)}, f32[128]{0:T(128)}, u32[]{:S(2)}) copy-start(f32[128]{0:T(128)} %param.29) | copy-start | bytes 1540
  120.1 42.6 %all-to-all-start = ((f32[16,4,64,128]{3,2,1,0:T(8,128)}), f32[16,4,64,128]{3,2,1,0:T(8,128)S(1)}, u32[]{:S(2)}, u32[]{:S(2)}) async-start(f32[16,4,64,128]{3,2,1,0:T(8,128)} %stack.13), calls=%async_computation | async-start | bytes 4194304 | tf_op jit(solution)/shard_map/all_to_all | solution.py:74
  135.2 28.7 %copy-start.11 = (bf16[4,4]{1,0:T(4,128)(2,1)S(1)}, bf16[4,4]{1,0:T(4,128)(2,1)}, u32[]{:S(2)}) copy-start(bf16[4,4]{1,0:T(4,128)(2,1)} %param.25) | copy-start | bytes 100
  135.2 28.7 %copy-start.12 = (f32[4]{0:T(128)S(1)}, f32[4]{0:T(128)}, u32[]{:S(2)}) copy-start(f32[4]{0:T(128)} %param.31) | copy-start | bytes 52
  135.2 29.0 %copy-start.7 = (bf16[4,4]{1,0:T(4,128)(2,1)S(1)}, bf16[4,4]{1,0:T(4,128)(2,1)}, u32[]{:S(2)}) copy-start(bf16[4,4]{1,0:T(4,128)(2,1)} %param.28) | copy-start | bytes 100
  135.2 96.9 %all-gather.5.cloned.1.call-start = ((), (), s32[]{:S(2)}) async-start(), calls=%async_computation.3 | async-start | bytes 2228224 | tf_op jit(solution)/shard_map/all_gather | solution.py:35
  135.4 96.8 %copy-start.10 = (bf16[64,2048]{1,0:T(8,128)(2,1)S(1)}, bf16[64,2048]{1,0:T(8,128)(2,1)}, u32[]{:S(2)}) copy-start(bf16[64,2048]{1,0:T(8,128)(2,1)} %param.27) | copy-start | bytes 786436
  234.5 41.5 %copy-start.2 = (bf16[128,2048]{1,0:T(8,128)(2,1)S(1)}, bf16[128,2048]{1,0:T(8,128)(2,1)}, u32[]{:S(2)}) copy-start(bf16[128,2048]{1,0:T(8,128)(2,1)} %param.26) | copy-start | bytes 1572868
Sparse Core Ops, SparseCore 0:
  46.1 70.3 all-gather.2
  170.1 62.0 all-gather.4
